TPU v7x, 128 devices: a whole 4x4x4 slice. The times are simulated.
128 devices in a mesh: dp: 16 (over x, y), tensor: 8 (over z, core).
Axes of the slice: x: 4, y: 4, z: 4, core: 2. Of those that a mesh axis runs over, the one named last changes fastest.
Arguments:
- kv_part: bfloat16 [8, 4096, 12288], P('tensor', 'dp'), may hold values from -2 to 2
- queries: bfloat16 [8192, 6144], P('dp', 'tensor'), may hold values from -6 to 6
- w_out: bfloat16 [6144, 8192], P('tensor'), may hold values from -0.078125 to 0.078125
- d_out: bfloat16 [8192, 8192], P('dp', 'tensor'), may hold values from -48 to 48
- nbr_owner: int32 [128, 2], replicated, may hold values from 0 to 15, as said below
- nbr_slot: int32 [128, 2], replicated, may hold values from 0 to 1, as said below
Outputs:
- mixed: bfloat16 [8192, 8192], P('dp', 'tensor')
- d_kv: bfloat16 [4096, 12288], P('dp', 'tensor')
Inputs may be any that keep to these rules, and one draw needn't show every extreme that they name: `nbr_owner`: the two neighbours of one span have different owners. `nbr_slot`: all neighbours that the spans of one dp index r (spans r * 8 to (r + 1) * 8 - 1) take from one owner have the same slot.
All inputs are finite; a program needn't handle non-finite values.
Results may differ from a plain program's by a relative error of at most 0.025.
Values may be sent and summed in bfloat16 or wider, within the bound.
A program may use at most 192 MiB of HBM per device.

v0:
```python
import jax
import jax.numpy as jnp
from jax import lax
from jax.sharding import PartitionSpec as P

HD = 128
SPAN = 64
NBR_LEN = 128
NB_DEV = 2


def local(kv_part, queries, w_out, d_out, nbr_owner, nbr_slot):
    dp_count = lax.axis_size("dp")
    reader = lax.axis_index("dp")
    head_width = w_out.shape[0]
    heads_here = head_width // HD
    share_width = 2 * head_width
    span_count = queries.shape[0] // SPAN
    read_count = 2 * span_count
    block_width = NBR_LEN * share_width
    local_partial = kv_part[0]
    summed = lax.psum(local_partial, "tensor").astype(jnp.float32)
    shares = lax.dynamic_slice_in_dim(
        summed, lax.axis_index("tensor") * share_width, share_width, 1
    ).astype(jnp.bfloat16)
    share_blocks = shares.reshape(NB_DEV, block_width)
    owner_ids = jnp.arange(dp_count, dtype=jnp.int32)
    slot_ids = jnp.arange(NB_DEV, dtype=jnp.int32)
    owner_hits = nbr_owner[:, :, None] == owner_ids[None, None, :]
    per_reader = owner_hits.reshape(dp_count, read_count, dp_count)
    reads_from = jnp.any(per_reader, axis=1)
    slot_from = jnp.max(jnp.where(per_reader, nbr_slot.reshape(dp_count, read_count, 1), 0), axis=1)
    my_owner = lax.dynamic_slice_in_dim(nbr_owner, reader * span_count, span_count, 0).reshape(
        read_count
    )
    my_slot = lax.dynamic_slice_in_dim(nbr_slot, reader * span_count, span_count, 0).reshape(
        read_count
    )
    read_table = (my_owner[:, None] == owner_ids[None, :]).astype(jnp.bfloat16)
    serving = lax.dynamic_index_in_dim(reads_from, reader, 1, False)
    serving_slot = lax.dynamic_index_in_dim(slot_from, reader, 1, False)
    owner_select = ((serving_slot[:, None] == slot_ids[None, :]) & serving[:, None]).astype(
        jnp.bfloat16
    )
    everyone = lax.all_gather(share_blocks, "dp", axis=0, tiled=True)
    wanted = (my_owner * NB_DEV + my_slot)[:, None] == jnp.arange(
        dp_count * NB_DEV, dtype=jnp.int32
    )[None, :]
    neighbours = jnp.dot(
        wanted.astype(jnp.bfloat16), everyone, preferred_element_type=jnp.float32
    ).astype(jnp.bfloat16)
    layout = neighbours.reshape(span_count, 2 * NBR_LEN, heads_here, 2, HD)
    keys = layout[:, :, :, 0]
    values = layout[:, :, :, 1]
    query_view = queries.reshape(span_count, SPAN, heads_here, HD)
    factor = HD ** (-0.5)
    scores = (
        jnp.einsum("cqhd,ckhd->chqk", query_view, keys, preferred_element_type=jnp.float32) * factor
    )
    highest = jnp.max(scores, axis=-1, keepdims=True)
    expo = jnp.exp(scores - highest)
    probs = expo / jnp.sum(expo, axis=-1, keepdims=True)
    probs_low = probs.astype(jnp.bfloat16)
    attended = jnp.einsum("chqk,ckhd->cqhd", probs_low, values, preferred_element_type=jnp.float32)
    attended = attended.astype(jnp.bfloat16).reshape(span_count * SPAN, head_width)
    partial_out = jnp.dot(attended, w_out, preferred_element_type=jnp.float32)
    mixed = lax.psum_scatter(
        partial_out.astype(jnp.bfloat16), "tensor", scatter_dimension=1, tiled=True
    )
    grad_attended = lax.dot_general(
        lax.all_gather(d_out, "tensor", axis=1, tiled=True),
        w_out,
        (((1,), (1,)), ((), ())),
        preferred_element_type=jnp.float32,
    ).astype(jnp.bfloat16)
    grad_view = grad_attended.reshape(span_count, SPAN, heads_here, HD)
    grad_values = jnp.einsum(
        "chqk,cqhd->ckhd", probs_low, grad_view, preferred_element_type=jnp.float32
    )
    grad_probs = jnp.einsum(
        "cqhd,ckhd->chqk", grad_view, values, preferred_element_type=jnp.float32
    )
    grad_scores = probs * (grad_probs - jnp.sum(probs * grad_probs, axis=-1, keepdims=True))
    grad_scores = grad_scores.astype(jnp.bfloat16)
    grad_keys = (
        jnp.einsum("chqk,cqhd->ckhd", grad_scores, query_view, preferred_element_type=jnp.float32)
        * factor
    )
    grad_blocks = jnp.stack([grad_keys, grad_values], axis=3).reshape(read_count, block_width)
    per_owner = lax.dot_general(
        read_table.astype(jnp.float32),
        grad_blocks,
        (((0,), (0,)), ((), ())),
        precision=lax.Precision.HIGHEST,
        preferred_element_type=jnp.float32,
    ).astype(jnp.bfloat16)
    returned = lax.all_to_all(per_owner, "dp", split_axis=0, concat_axis=0, tiled=True)
    owner_grad = lax.dot_general(
        owner_select, returned, (((0,), (0,)), ((), ())), preferred_element_type=jnp.float32
    )
    d_kv = owner_grad.astype(jnp.bfloat16).reshape(NB_DEV * NBR_LEN, share_width)
    return (mixed, d_kv)


def solution(mesh):
    placed = (
        P("tensor", "dp", None),
        P("dp", "tensor"),
        P("tensor", None),
        P("dp", "tensor"),
        P(),
        P(),
    )
    return jax.shard_map(
        local,
        mesh=mesh,
        in_specs=placed,
        out_specs=(P("dp", "tensor"), P("dp", "tensor")),
        check_vma=False,
    )
```

profile of v0, /device:TPU:28, one launch (start us, length us, event | category | flops | bytes accessed | tf_op | source)
XLA Modules:
  0.0 541.4 jit_solution(5792027820581872935)
XLA Ops:
  8.0 89.0 %all-reduce.2.cloned.1.call-done = bf16[256,12288]{1,0:T(8,128)(2,1)} async-done(((bf16[256,12288]{1,0:T(8,128)(2,1)}), bf16[256,12288]{1,0:T(8,128)(2,1)}) %all-reduce.2.cloned.1.call-update) | async-done | bytes 6291472 | tf_op jit(solution)/shard_map/psum | solution.py:22
  102.8 85.0 %all-gather.6.cloned.1.call-done = bf16[16,2,196608]{2,1,0:T(2,128)(2,1)} async-done(((bf16[1,2,196608]{2,1,0:T(2,128)(2,1)}), bf16[16,2,196608]{2,1,0:T(2,128)(2,1)}) %all-gather.6.cloned.1.call-update) | async-done | bytes 12582928 | tf_op jit(solution)/shard_map/all_gather | solution.py:45
  187.7 11.3 %reshape.63 = bf16[32,196608]{1,0:T(8,128)(2,1)} reshape(bf16[16,2,196608]{2,1,0:T(2,128)(2,1)} %all-gather.6.cloned.1.call-done) | data formatting | bytes 25165824
  199.0 10.4 %convolution_convert_fusion.1 = bf16[16,196608]{1,0:T(8,128)(2,1)} fusion(bf16[32,196608]{1,0:T(8,128)(2,1)} %reshape.63, s32[16]{0:T(128)S(1)} %multiply_add_fusion), kind=kOutput, calls=%fused_computation.2 | convolution fusion | flops 204472832 | bytes 18874432 | tf_op jit(solution)/shard_map/dot_general | solution.py:49
  209.4 9.9 %reshape.56 = bf16[8,256,6,2,128]{4,3,2,1,0:T(2,128)(2,1)} reshape(bf16[16,196608]{1,0:T(8,128)(2,1)} %convolution_convert_fusion.1) | data formatting | bytes 12582912 | tf_op jit(solution)/shard_map/reshape | solution.py:52
  219.3 13.7 %fusion.42 = (bf16[8,256,6,1,128]{4,3,2,1,0:T(2,128)(2,1)S(1)}, bf16[8,256,6,1,128]{4,3,2,1,0:T(2,128)(2,1)}) fusion(bf16[8,256,6,2,128]{4,3,2,1,0:T(2,128)(2,1)} %reshape.56), kind=kLoop, calls=%fused_computation.54 | loop fusion | bytes 12582912 | tf_op jit(solution)/shard_map/slice | solution.py:53
  234.2 2.3 fusion.43
  236.5 9.2 %fusion.12 = bf16[8,64,6,128]{3,1,2,0:T(8,128)(2,1)} fusion(bf16[8,256,6,1,128]{4,3,2,1,0:T(2,128)(2,1)} %get-tuple-element.3, f32[8,6,64]{2,1,0:T(8,128)S(1)} %get-tuple-element.4, f32[8,6,256,64]{2,3,1,0:T(8,128)S(1)} %fusion.4), kind=kOutput, calls=%fused_computation.27 | convolution fusion | flops 205655296 | bytes 7090176 | tf_op jit(solution)/shard_map/chqk,ckhd->cqhd/dot_general | solution.py:64
  247.4 13.4 %convolution_convert_fusion.3 = bf16[512,8192]{1,0:T(8,128)(2,1)} fusion(bf16[768,8192]{1,0:T(8,128)(2,1)} %param.8, bf16[64,8,6,128]{3,2,1,0:T(8,128)(2,1)S(1)} %bitcast.71), kind=kOutput, calls=%fused_computation.6 | convolution fusion | flops 6446645248 | bytes 21757952 | tf_op jit(solution)/shard_map/dot_general | solution.py:66
  260.9 13.5 %convolution_convert_fusion.5 = bf16[512,768]{1,0:T(8,128)(2,1)} fusion(bf16[512,8192]{1,0:T(8,128)(2,1)} %all-gather.4.cloned.1.call-done, bf16[768,8192]{1,0:T(8,128)(2,1)} %param.8), kind=kOutput, calls=%fused_computation.26 | convolution fusion | flops 6442844160 | bytes 21757952 | tf_op jit(solution)/shard_map/dot_general | solution.py:70
  274.4 2.9 reshape.59
  277.3 10.3 %convolution_bitcast_fusion = f32[8,256,6,1,128]{4,1,2,0,3:T(8,128)} fusion(bf16[8,64,6,128]{3,2,1,0:T(8,128)(2,1)} %reshape.59, f32[8,6,64]{2,1,0:T(8,128)S(1)} %get-tuple-element.4, f32[8,6,256,64]{2,3,1,0:T(8,128)S(1)} %fusion.4), kind=kOutput, calls=%fused_computation.20 | convolution fusion | flops 205262080 | bytes 10235904 | tf_op jit(solution)/shard_map/chqk,cqhd->ckhd/dot_general | solution.py:77
  287.6 7.2 %multiply_reduce_fusion = (f32[8,6,64]{2,1,0:T(8,128)S(1)}, f32[8,6,64,256]{3,2,1,0:T(8,128)}) fusion(f32[8,6,64,256]{3,2,1,0:T(8,128)} %get-tuple-element.5, f32[8,6,64]{2,1,0:T(8,128)S(1)} %get-tuple-element.4, bf16[8,256,6,1,128]{4,3,2,1,0:T(2,128)(2,1)} %get-tuple-element.3, bf16[8,64,6,128]{3,2,1,0:T(8,128)(2,1)} %reshape.59), kind=kOutput, calls=%fused_computation.18 | convolution fusion | flops 203682816 | bytes 10248192 | tf_op jit(solution)/shard_map/cqhd,ckhd->chqk/dot_general | solution.py:80
  294.8 11.7 %multiply_bitcast_fusion = f32[8,256,6,1,128]{4,1,2,0,3:T(8,128)} fusion(f32[8,6,64,256]{3,2,1,0:T(8,128)} %get-tuple-element.7, f32[8,6,64]{2,1,0:T(8,128)S(1)} %get-tuple-element.6, bf16[8,64,6,128]{3,2,1,0:T(8,128)(2,1)} %reshape.57, f32[8,6,64]{2,1,0:T(8,128)S(1)} %get-tuple-element.4, f32[8,6,256,64]{2,3,1,0:T(8,128)S(1)} %fusion.4), kind=kOutput, calls=%fused_computation.9 | convolution fusion | flops 208407808 | bytes 13393920 | tf_op jit(solution)/shard_map/chqk,cqhd->ckhd/dot_general | solution.py:86
  306.5 10.9 %pad_maximum_fusion = f32[8,256,6,2,128]{4,1,2,0,3:T(8,128)} fusion(f32[8,256,6,1,128]{4,1,2,0,3:T(8,128)} %convolution_bitcast_fusion, f32[8,256,6,1,128]{4,1,2,0,3:T(8,128)} %multiply_bitcast_fusion), kind=kLoop, calls=%fused_computation.5 | loop fusion | flops 3145728 | bytes 25165824 | tf_op jit(solution)/shard_map/stack | solution.py:89
  317.4 22.2 %copy.84 = f32[8,256,6,2,128]{4,3,2,1,0:T(2,128)} copy(f32[8,256,6,2,128]{4,1,2,0,3:T(8,128)} %pad_maximum_fusion) | data formatting | bytes 25165824 | tf_op jit(solution)/shard_map/stack | solution.py:89
  339.6 21.3 %reshape.60 = f32[16,196608]{1,0:T(8,128)} reshape(f32[8,256,6,2,128]{4,3,2,1,0:T(2,128)} %copy.84) | data formatting | bytes 25165824 | tf_op jit(solution)/shard_map/reshape | solution.py:89
  360.9 10.9 %fusion.1 = bf16[16,1,196608]{2,0,1:T(8,128)(2,1)} fusion(f32[16,196608]{1,0:T(8,128)} %reshape.60, s32[16]{0:T(128)S(1)} %reshape.53), kind=kOutput, calls=%fused_computation.3 | convolution fusion | flops 607125760 | bytes 18874432 | tf_op jit(solution)/shard_map/dot_general | solution.py:90
  372.3 8.8 %reduce.4 = bf16[16,196608]{1,0:T(8,128)(2,1)} reduce(bf16[16,1,196608]{2,0,1:T(8,128)(2,1)} %fusion.1, bf16[]{:T(256)} %broadcast.20), dimensions={1}, to_apply=%copy.85.reduce_sub_computation | reduce | bytes 12582914 | tf_op jit(solution)/shard_map/all_to_all | solution.py:97
  381.2 9.3 %reshape.67 = bf16[16,2,98304]{2,1,0:T(2,128)(2,1)} reshape(bf16[16,196608]{1,0:T(8,128)(2,1)} %reduce.4) | data formatting | bytes 12582912
  390.5 7.2 %all-to-all-start = ((bf16[16,2,98304]{2,1,0:T(2,128)(2,1)}), bf16[16,2,98304]{2,1,0:T(2,128)(2,1)}, u32[]{:S(2)}, u32[]{:S(2)}) async-start(bf16[16,2,98304]{2,1,0:T(2,128)(2,1)} %reshape.67), calls=%async_computation.1 | async-start | bytes 12582912 | tf_op jit(solution)/shard_map/all_to_all | solution.py:97
  398.8 107.1 %all-to-all-done = bf16[16,2,98304]{2,1,0:T(2,128)(2,1)} async-done(((bf16[16,2,98304]{2,1,0:T(2,128)(2,1)}), bf16[16,2,98304]{2,1,0:T(2,128)(2,1)}, u32[]{:S(2)}, u32[]{:S(2)}) %all-to-all-start) | async-done | bytes 6291488 | tf_op jit(solution)/shard_map/all_to_all | solution.py:97
  505.9 14.3 %reshape.68 = bf16[16,1,196608]{2,1,0:T(2,128)(2,1)} reshape(bf16[16,2,98304]{2,1,0:T(2,128)(2,1)} %all-to-all-done) | data formatting | bytes 12582912
  520.2 12.8 %convolution_convert_fusion.2 = bf16[2,196608]{1,0:T(2,128)(2,1)S(1)} fusion(bf16[16,1,196608]{2,1,0:T(2,128)(2,1)} %reshape.68, s32[16]{0:T(128)S(1)} %dynamic-slice_reduce_fusion, pred[16]{0:T(512)(128)(4,1)S(1)} %dynamic-slice_reduce_fusion.1), kind=kOutput, calls=%fused_computation.4 | convolution fusion | flops 12976192 | bytes 7077968 | tf_op jit(solution)/shard_map/dot_general | solution.py:98
  (39 shorter events, 12.6 us)
Async XLA Ops:
  7.2 89.8 %all-reduce.2.cloned.1.call-start = ((), (), s32[]{:S(2)}) async-start(), calls=%async_computation.2 | async-start | bytes 12582912 | tf_op jit(solution)/shard_map/psum | solution.py:22
  7.9 92.6 %copy-start.2 = (s32[128,2]{0,1:T(2,128)S(1)}, s32[128,2]{0,1:T(2,128)}, u32[]{:S(2)}) copy-start(s32[128,2]{0,1:T(2,128)} %param.11) | copy-start | bytes 3076
  7.9 92.6 %copy-start.3 = (s32[128,2]{0,1:T(2,128)S(1)}, s32[128,2]{0,1:T(2,128)}, u32[]{:S(2)}) copy-start(s32[128,2]{0,1:T(2,128)} %param.10) | copy-start | bytes 3076
  7.9 93.0 %copy-start.1 = (bf16[512,768]{1,0:T(8,128)(2,1)S(1)}, bf16[512,768]{1,0:T(8,128)(2,1)}, u32[]{:S(2)}) copy-start(bf16[512,768]{1,0:T(8,128)(2,1)} %param.7) | copy-start | bytes 2359300
  7.9 179.8 %all-gather.6.cloned.1.call-start = ((), (), s32[]{:S(2)}) async-start(), calls=%async_computation.5 | async-start | bytes 13369344 | tf_op jit(solution)/shard_map/all_gather | solution.py:45
  99.7 161.2 %all-gather.4.cloned.1.call-start = ((), (), s32[]{:S(2)}) async-start(), calls=%async_computation.4 | async-start | bytes 9437184 | tf_op jit(solution)/shard_map/all_gather | solution.py:71
  100.4 434.3 %reduce-scatter.2.cloned.1.call-start = ((), (), s32[]{:S(2)}) async-start(), calls=%async_computation.3 | async-start | bytes 9437184 | tf_op jit(solution)/shard_map/reduce_scatter | solution.py:67
  219.3 13.7 %copy-start = (bf16[8,64,6,128]{3,2,1,0:T(8,128)(2,1)S(1)}, bf16[8,64,6,128]{3,2,1,0:T(8,128)(2,1)}, u32[]{:S(2)}) copy-start(bf16[8,64,6,128]{3,2,1,0:T(8,128)(2,1)} %reshape.57) | copy-start | bytes 2359300
  390.5 115.4 %all-to-all-start = ((bf16[16,2,98304]{2,1,0:T(2,128)(2,1)}), bf16[16,2,98304]{2,1,0:T(2,128)(2,1)}, u32[]{:S(2)}, u32[]{:S(2)}) async-start(bf16[16,2,98304]{2,1,0:T(2,128)(2,1)} %reshape.67), calls=%async_computation.1 | async-start | bytes 12582912 | tf_op jit(solution)/shard_map/all_to_all | solution.py:97
Sparse Core Ops, SparseCore 0:
  10.4 86.5 all-reduce.1
  99.8 87.8 all-gather.5
  189.4 51.1 all-gather.3
  261.0 53.9 reduce-scatter.1
where the time goes:
time: 549 us; the launch traced here: 541 us
  waiting for transfers between devices  283 us (52%)
  local copies, waits for them, and re-layouts  113 us (21%)
  matrix products  101 us (18%)
  other arithmetic  23.6 us (4%)
  between operations  14.1 us (3%)
  starting transfers between devices  7.38 us (1%)
    all_to_all x1, waiting for transfers between devices, local(): lax.all_to_all(per_owner, 'dp', split_axis=0, concat_axis=0, tiled=True)  107 us
    psum x1, waiting for transfers between devices, local(): summed = lax.psum(local_partial, 'tensor').astype(jnp.float32)  89 us
    all_gather x1, waiting for transfers between devices, local(): everyone = lax.all_gather(share_blocks, 'dp', axis=0, tiled=True)  85 us
    unnamed x14, local copies, waits for them, and re-layouts  36.7 us
    another operation x1, local copies, waits for them, and re-layouts, local(): jnp.stack([grad_keys, grad_values], axis=3).reshape(read_count, block_width)  22.2 us
    reshape x1, local copies, waits for them, and re-layouts, local(): jnp.stack([grad_keys, grad_values], axis=3).reshape(read_count, block_width)  21.3 us
    slice x1, local copies, waits for them, and re-layouts, local(): keys = layout[:, :, :, 0]  13.7 us
    dot_general x1, matrix products, local(): lax.dot_general(lax.all_gather(d_out, 'tensor', axis=1, tiled=True), w_ou...  13.5 us
  transfers between devices with their start and end apart: 5, of which 3 were waited for; matrix products, arithmetic and copies ran while one was open for 43% of the time, Pallas kernels for 0%

commit v1 on v0

--- a/solution.py
+++ b/solution.py
@@ -1,3 +1,4 @@
+import functools
 import jax
 import jax.numpy as jnp
 from jax import lax
@@ -7,6 +8,14 @@
 SPAN = 64
 NBR_LEN = 128
 NB_DEV = 2
+
+
+def _get_area(x_part, axis_id):
+    current_block = lax.all_gather(x_part, axis_name=axis_id)
+    return jnp.sum(current_block, 0)
+
+
+advance_routes_all = functools.partial(_get_area, axis_id="tensor")
 
 
 def local(kv_part, queries, w_out, d_out, nbr_owner, nbr_slot):
@@ -19,7 +28,7 @@
     read_count = 2 * span_count
     block_width = NBR_LEN * share_width
     local_partial = kv_part[0]
-    summed = lax.psum(local_partial, "tensor").astype(jnp.float32)
+    summed = advance_routes_all(local_partial).astype(jnp.float32)
     shares = lax.dynamic_slice_in_dim(
         summed, lax.axis_index("tensor") * share_width, share_width, 1
     ).astype(jnp.bfloat16)

time: 549 us -> 712 us (1.30)
  waiting for transfers between devices: 283 us -> 425 us
  other arithmetic: 23.6 us -> 43.6 us
    all_gather x0 -> x1, waiting for transfers between devices: none -> 231 us  [_get_area(): current_block = lax.all_gather(x_part, axis_name=axis_id)]
    psum x1 -> x0, waiting for transfers between devices: 89 us -> none  [local(): summed = lax.psum(local_partial, 'tensor').astype(jnp.float32)]
    reduce_sum x0 -> x1, other arithmetic: none -> 20 us  [_get_area(): return jnp.sum(current_block, 0)]
  transfers between devices with their start and end apart: 5 -> 5, of which waited for: 3 -> 3; matrix products, arithmetic and copies ran while one was open for 43% -> 33% of each run, Pallas kernels for 0% -> 0%
where the time goes in v1:
time: 712 us; the launch traced here: 704 us
  waiting for transfers between devices  425 us (60%)
  local copies, waits for them, and re-layouts  113 us (16%)
  matrix products  101 us (14%)
  other arithmetic  43.6 us (6%)
  between operations  14.1 us (2%)
  starting transfers between devices  7.4 us (1%)
    all_gather x1, waiting for transfers between devices, _get_area(): current_block = lax.all_gather(x_part, axis_name=axis_id)  231 us
    all_to_all x1, waiting for transfers between devices, local(): lax.all_to_all(per_owner, 'dp', split_axis=0, concat_axis=0, tiled=True)  107 us
    all_gather x1, waiting for transfers between devices, local(): everyone = lax.all_gather(share_blocks, 'dp', axis=0, tiled=True)  84.9 us
    unnamed x14, local copies, waits for them, and re-layouts  36.7 us
    another operation x1, local copies, waits for them, and re-layouts, local(): jnp.stack([grad_keys, grad_values], axis=3).reshape(read_count, block_width)  22.2 us
    reshape x1, local copies, waits for them, and re-layouts, local(): jnp.stack([grad_keys, grad_values], axis=3).reshape(read_count, block_width)  21.3 us
    reduce_sum x1, other arithmetic, _get_area(): return jnp.sum(current_block, 0)  20 us
  transfers between devices with their start and end apart: 5, of which 3 were waited for; matrix products, arithmetic and copies ran while one was open for 33% of the time, Pallas kernels for 0%

profile of v1, /device:TPU:28, one launch (start us, length us, event | category | flops | bytes accessed | tf_op | source)
XLA Modules:
  0.0 703.6 jit_solution(5656104867991589531)
XLA Ops:
  7.9 231.2 %all-gather.5.cloned.1.call-done = bf16[8,256,12288]{2,1,0:T(8,128)(2,1)} async-done(((bf16[1,256,12288]{2,1,0:T(8,128)(2,1)}), bf16[8,256,12288]{2,1,0:T(8,128)(2,1)}) %all-gather.5.cloned.1.call-update) | async-done | bytes 50331664 | tf_op jit(solution)/shard_map/all_gather | solution.py:14
  239.1 20.0 %reduce_sum.30 = bf16[256,12288]{1,0:T(8,128)(2,1)} reduce(bf16[8,256,12288]{2,1,0:T(8,128)(2,1)} %all-gather.5.cloned.1.call-done, bf16[]{:T(256)} %constant.11.clone.1), dimensions={0}, to_apply=%region_0.0 | reduce | flops 22020096 | bytes 56623104 | tf_op jit(solution)/shard_map/reduce_sum | solution.py:15
  265.0 84.9 %all-gather.9.cloned.1.call-done = bf16[16,2,196608]{2,1,0:T(2,128)(2,1)} async-done(((bf16[1,2,196608]{2,1,0:T(2,128)(2,1)}), bf16[16,2,196608]{2,1,0:T(2,128)(2,1)}) %all-gather.9.cloned.1.call-update) | async-done | bytes 12582928 | tf_op jit(solution)/shard_map/all_gather | solution.py:54
  349.9 11.3 %reshape.63 = bf16[32,196608]{1,0:T(8,128)(2,1)} reshape(bf16[16,2,196608]{2,1,0:T(2,128)(2,1)} %all-gather.9.cloned.1.call-done) | data formatting | bytes 25165824
  361.2 10.4 %convolution_convert_fusion.1 = bf16[16,196608]{1,0:T(8,128)(2,1)} fusion(bf16[32,196608]{1,0:T(8,128)(2,1)} %reshape.63, s32[16]{0:T(128)S(1)} %multiply_add_fusion), kind=kOutput, calls=%fused_computation.2 | convolution fusion | flops 204472832 | bytes 18874432 | tf_op jit(solution)/shard_map/dot_general | solution.py:58
  371.6 9.9 %reshape.56 = bf16[8,256,6,2,128]{4,3,2,1,0:T(2,128)(2,1)} reshape(bf16[16,196608]{1,0:T(8,128)(2,1)} %convolution_convert_fusion.1) | data formatting | bytes 12582912 | tf_op jit(solution)/shard_map/reshape | solution.py:61
  381.5 13.7 %fusion.42 = (bf16[8,256,6,1,128]{4,3,2,1,0:T(2,128)(2,1)S(1)}, bf16[8,256,6,1,128]{4,3,2,1,0:T(2,128)(2,1)}) fusion(bf16[8,256,6,2,128]{4,3,2,1,0:T(2,128)(2,1)} %reshape.56), kind=kLoop, calls=%fused_computation.54 | loop fusion | bytes 12582912 | tf_op jit(solution)/shard_map/slice | solution.py:62
  398.7 9.2 %fusion.12 = bf16[8,64,6,128]{3,1,2,0:T(8,128)(2,1)} fusion(bf16[8,256,6,1,128]{4,3,2,1,0:T(2,128)(2,1)} %get-tuple-element.3, f32[8,6,64]{2,1,0:T(8,128)S(1)} %get-tuple-element.4, f32[8,6,256,64]{2,3,1,0:T(8,128)S(1)} %fusion.4), kind=kOutput, calls=%fused_computation.27 | convolution fusion | flops 205655296 | bytes 7090176 | tf_op jit(solution)/shard_map/chqk,ckhd->cqhd/dot_general | solution.py:73
  409.6 13.4 %convolution_convert_fusion.3 = bf16[512,8192]{1,0:T(8,128)(2,1)} fusion(bf16[768,8192]{1,0:T(8,128)(2,1)} %param.8, bf16[64,8,6,128]{3,2,1,0:T(8,128)(2,1)S(1)} %bitcast.69), kind=kOutput, calls=%fused_computation.6 | convolution fusion | flops 6446645248 | bytes 21757952 | tf_op jit(solution)/shard_map/dot_general | solution.py:75
  423.1 13.5 %convolution_convert_fusion.5 = bf16[512,768]{1,0:T(8,128)(2,1)} fusion(bf16[512,8192]{1,0:T(8,128)(2,1)} %all-gather.7.cloned.1.call-done, bf16[768,8192]{1,0:T(8,128)(2,1)} %param.8), kind=kOutput, calls=%fused_computation.26 | convolution fusion | flops 6442844160 | bytes 21757952 | tf_op jit(solution)/shard_map/dot_general | solution.py:79
  436.6 2.9 reshape.59
  439.5 10.3 %convolution_bitcast_fusion = f32[8,256,6,1,128]{4,1,2,0,3:T(8,128)} fusion(bf16[8,64,6,128]{3,2,1,0:T(8,128)(2,1)} %reshape.59, f32[8,6,64]{2,1,0:T(8,128)S(1)} %get-tuple-element.4, f32[8,6,256,64]{2,3,1,0:T(8,128)S(1)} %fusion.4), kind=kOutput, calls=%fused_computation.20 | convolution fusion | flops 205262080 | bytes 10235904 | tf_op jit(solution)/shard_map/chqk,cqhd->ckhd/dot_general | solution.py:86
  449.8 7.2 %multiply_reduce_fusion = (f32[8,6,64]{2,1,0:T(8,128)S(1)}, f32[8,6,64,256]{3,2,1,0:T(8,128)}) fusion(f32[8,6,64,256]{3,2,1,0:T(8,128)} %get-tuple-element.5, f32[8,6,64]{2,1,0:T(8,128)S(1)} %get-tuple-element.4, bf16[8,256,6,1,128]{4,3,2,1,0:T(2,128)(2,1)} %get-tuple-element.3, bf16[8,64,6,128]{3,2,1,0:T(8,128)(2,1)} %reshape.59), kind=kOutput, calls=%fused_computation.18 | convolution fusion | flops 203682816 | bytes 10248192 | tf_op jit(solution)/shard_map/cqhd,ckhd->chqk/dot_general | solution.py:89
  457.0 11.7 %multiply_bitcast_fusion = f32[8,256,6,1,128]{4,1,2,0,3:T(8,128)} fusion(f32[8,6,64,256]{3,2,1,0:T(8,128)} %get-tuple-element.7, f32[8,6,64]{2,1,0:T(8,128)S(1)} %get-tuple-element.6, bf16[8,64,6,128]{3,2,1,0:T(8,128)(2,1)} %reshape.57, f32[8,6,64]{2,1,0:T(8,128)S(1)} %get-tuple-element.4, f32[8,6,256,64]{2,3,1,0:T(8,128)S(1)} %fusion.4), kind=kOutput, calls=%fused_computation.9 | convolution fusion | flops 208407808 | bytes 13393920 | tf_op jit(solution)/shard_map/chqk,cqhd->ckhd/dot_general | solution.py:95
  468.7 10.9 %pad_maximum_fusion = f32[8,256,6,2,128]{4,1,2,0,3:T(8,128)} fusion(f32[8,256,6,1,128]{4,1,2,0,3:T(8,128)} %convolution_bitcast_fusion, f32[8,256,6,1,128]{4,1,2,0,3:T(8,128)} %multiply_bitcast_fusion), kind=kLoop, calls=%fused_computation.5 | loop fusion | flops 3145728 | bytes 25165824 | tf_op jit(solution)/shard_map/stack | solution.py:98
  479.6 22.2 %copy.84 = f32[8,256,6,2,128]{4,3,2,1,0:T(2,128)} copy(f32[8,256,6,2,128]{4,1,2,0,3:T(8,128)} %pad_maximum_fusion) | data formatting | bytes 25165824 | tf_op jit(solution)/shard_map/stack | solution.py:98
  501.8 21.3 %reshape.60 = f32[16,196608]{1,0:T(8,128)} reshape(f32[8,256,6,2,128]{4,3,2,1,0:T(2,128)} %copy.84) | data formatting | bytes 25165824 | tf_op jit(solution)/shard_map/reshape | solution.py:98
  523.1 10.9 %fusion.1 = bf16[16,1,196608]{2,0,1:T(8,128)(2,1)} fusion(f32[16,196608]{1,0:T(8,128)} %reshape.60, s32[16]{0:T(128)S(1)} %reshape.53), kind=kOutput, calls=%fused_computation.3 | convolution fusion | flops 607125760 | bytes 18874432 | tf_op jit(solution)/shard_map/dot_general | solution.py:99
  534.5 8.8 %reduce.5 = bf16[16,196608]{1,0:T(8,128)(2,1)} reduce(bf16[16,1,196608]{2,0,1:T(8,128)(2,1)} %fusion.1, bf16[]{:T(256)} %broadcast.20), dimensions={1}, to_apply=%copy.85.reduce_sub_computation | reduce | bytes 12582914 | tf_op jit(solution)/shard_map/all_to_all | solution.py:106
  543.4 9.3 %reshape.67 = bf16[16,2,98304]{2,1,0:T(2,128)(2,1)} reshape(bf16[16,196608]{1,0:T(8,128)(2,1)} %reduce.5) | data formatting | bytes 12582912
  552.7 7.2 %all-to-all-start = ((bf16[16,2,98304]{2,1,0:T(2,128)(2,1)}), bf16[16,2,98304]{2,1,0:T(2,128)(2,1)}, u32[]{:S(2)}, u32[]{:S(2)}) async-start(bf16[16,2,98304]{2,1,0:T(2,128)(2,1)} %reshape.67), calls=%async_computation.1 | async-start | bytes 12582912 | tf_op jit(solution)/shard_map/all_to_all | solution.py:106
  561.0 107.1 %all-to-all-done = bf16[16,2,98304]{2,1,0:T(2,128)(2,1)} async-done(((bf16[16,2,98304]{2,1,0:T(2,128)(2,1)}), bf16[16,2,98304]{2,1,0:T(2,128)(2,1)}, u32[]{:S(2)}, u32[]{:S(2)}) %all-to-all-start) | async-done | bytes 6291488 | tf_op jit(solution)/shard_map/all_to_all | solution.py:106
  668.1 14.3 %reshape.68 = bf16[16,1,196608]{2,1,0:T(2,128)(2,1)} reshape(bf16[16,2,98304]{2,1,0:T(2,128)(2,1)} %all-to-all-done) | data formatting | bytes 12582912
  682.4 12.8 %convolution_convert_fusion.2 = bf16[2,196608]{1,0:T(2,128)(2,1)S(1)} fusion(bf16[16,1,196608]{2,1,0:T(2,128)(2,1)} %reshape.68, s32[16]{0:T(128)S(1)} %dynamic-slice_reduce_fusion, pred[16]{0:T(512)(128)(4,1)S(1)} %dynamic-slice_reduce_fusion.1), kind=kOutput, calls=%fused_computation.4 | convolution fusion | flops 12976192 | bytes 7077968 | tf_op jit(solution)/shard_map/dot_general | solution.py:107
  (40 shorter events, 15.0 us)
Async XLA Ops:
  7.2 232.0 %all-gather.5.cloned.1.call-start = ((), (), s32[]{:S(2)}) async-start(), calls=%async_computation.2 | async-start | bytes 56623104 | tf_op jit(solution)/shard_map/all_gather | solution.py:14
  7.9 342.0 %all-gather.9.cloned.1.call-start = ((), (), s32[]{:S(2)}) async-start(), calls=%async_computation.5 | async-start | bytes 13369344 | tf_op jit(solution)/shard_map/all_gather | solution.py:54
  259.1 3.5 copy-start.2
  259.1 3.5 copy-start.3
  259.2 4.0 copy-start.1
  261.9 161.2 %all-gather.7.cloned.1.call-start = ((), (), s32[]{:S(2)}) async-start(), calls=%async_computation.4 | async-start | bytes 9437184 | tf_op jit(solution)/shard_map/all_gather | solution.py:80
  262.6 434.3 %reduce-scatter.2.cloned.1.call-start = ((), (), s32[]{:S(2)}) async-start(), calls=%async_computation.3 | async-start | bytes 9437184 | tf_op jit(solution)/shard_map/reduce_scatter | solution.py:76
  381.5 13.7 %copy-start = (bf16[8,64,6,128]{3,2,1,0:T(8,128)(2,1)S(1)}, bf16[8,64,6,128]{3,2,1,0:T(8,128)(2,1)}, u32[]{:S(2)}) copy-start(bf16[8,64,6,128]{3,2,1,0:T(8,128)(2,1)} %reshape.57) | copy-start | bytes 2359300
  552.7 115.4 %all-to-all-start = ((bf16[16,2,98304]{2,1,0:T(2,128)(2,1)}), bf16[16,2,98304]{2,1,0:T(2,128)(2,1)}, u32[]{:S(2)}, u32[]{:S(2)}) async-start(bf16[16,2,98304]{2,1,0:T(2,128)(2,1)} %reshape.67), calls=%async_computation.1 | async-start | bytes 12582912 | tf_op jit(solution)/shard_map/all_to_all | solution.py:106
Sparse Core Ops, SparseCore 0:
  9.7 229.4 all-gather.4
  262.0 87.8 all-gather.8
  351.6 51.1 all-gather.6
  423.2 53.9 reduce-scatter.1
